TPU v7x, 32 devices: a whole 2x2x4 slice. The times are simulated.
32 devices in a mesh: fsdp: 16 (over z, x, core), dp: 2 (over y).
Axes of the slice: x: 2, y: 2, z: 4, core: 2. Of those that a mesh axis runs over, the one named last changes fastest.
Arguments:
- inputs: bfloat16 [6144, 4096], P(('fsdp', 'dp')), may hold values from -6 to 6
- grad_out: bfloat16 [6144, 14336], P(('fsdp', 'dp')), may hold values from -0.009765625 to 0.009765625
- projection: bfloat16 [4096, 128], P('fsdp'), may hold values from -0.375 to 0.375
- moment: float32 [14336, 128], P('fsdp'), may hold values from -1.5 to 1.5
- second: float32 [14336, 128], P('fsdp'), may hold values from 0.0001 to 0.001
Outputs:
- update: bfloat16 [4096, 14336], P('fsdp')
- new_moment: float32 [14336, 128], P('fsdp')
- new_second: float32 [14336, 128], P('fsdp')
All inputs are finite; a program needn't handle non-finite values.
Results may differ from a plain program's by a relative error of at most 0.0051.
Values may be sent and summed in bfloat16 or wider, within the bound.
No kernel may reach another device: no remote copies, remote signals or barrier semaphores. Data moves between devices by JAX's collectives and lax.ppermute only.
A program may use at most 64 MiB of HBM per device.

v0:
```python
import jax
import jax.numpy as jnp
from jax import lax
from jax.sharding import PartitionSpec as P

STEP = 10


def adam_step(low_rank, moment, second):
    new_moment = 0.9 * moment + 0.1 * low_rank
    new_second = 0.999 * second + 0.001 * (low_rank * low_rank)
    first_fix = 1.0 - 0.9**STEP
    second_fix = 1.0 - 0.999**STEP
    normalized = (new_moment / first_fix / (jnp.sqrt(new_second / second_fix) + 1e-08)).astype(
        jnp.bfloat16
    )
    return (new_moment, new_second, normalized)


def local(inputs, grad_out, projection, moment, second):
    projected = jnp.dot(
        inputs,
        lax.all_gather(projection, "fsdp", axis=0, tiled=True),
        preferred_element_type=jnp.float32,
    ).astype(jnp.bfloat16)
    contract = (((0,), (0,)), ((), ()))
    whole = lax.dot_general(grad_out, projected, contract, preferred_element_type=jnp.float32)
    whole = lax.psum(whole, "dp")
    low_rank = lax.psum_scatter(whole, "fsdp", scatter_dimension=0, tiled=True)
    new_moment, new_second, normalized = adam_step(low_rank, moment, second)
    expand = (((1,), (1,)), ((), ()))
    update = lax.dot_general(
        projection,
        lax.all_gather(normalized, "fsdp", axis=0, tiled=True),
        expand,
        preferred_element_type=jnp.float32,
    ).astype(jnp.bfloat16)
    return (update, new_moment, new_second)


def solution(mesh):
    in_specs = (
        P(("fsdp", "dp"), None),
        P(("fsdp", "dp"), None),
        P("fsdp", None),
        P("fsdp", None),
        P("fsdp", None),
    )
    out_specs = (P("fsdp", None), P("fsdp", None), P("fsdp", None))
    return jax.shard_map(local, mesh=mesh, in_specs=in_specs, out_specs=out_specs, check_vma=False)
```

profile of v0, /device:TPU:0, one launch (start us, length us, event | category | flops | bytes accessed | tf_op | source)
XLA Modules:
  0.0 252.6 jit_solution(8466995799311963233)
XLA Ops:
  7.2 0.0 copy-start
  7.2 0.0 all-gather.3.cloned.1.call-start
  7.2 0.7 all-gather.3.cloned.1.call-update
  7.9 0.0 reduce-scatter.2.cloned.1.call-start
  8.0 42.8 %all-gather.3.cloned.1.call-done = bf16[4096,128]{1,0:T(8,128)(2,1)} async-done(((bf16[256,128]{1,0:T(8,128)(2,1)}), bf16[4096,128]{1,0:T(8,128)(2,1)}) %all-gather.3.cloned.1.call-update) | async-done | bytes 1048592 | tf_op jit(solution)/shard_map/all_gather | solution.py:23
  50.7 0.0 copy-done
  50.7 7.6 %convolution_bitcast_fusion = f32[14336,128]{0,1:T(8,128)} fusion(bf16[192,14336]{1,0:T(8,128)(2,1)} %param.6, bf16[192,4096]{1,0:T(8,128)(2,1)S(1)} %copy-done, bf16[4096,128]{1,0:T(8,128)(2,1)} %all-gather.3.cloned.1.call-done), kind=kOutput, calls=%fused_computation.2 | convolution fusion | flops 905994240 | bytes 15466496 | tf_op jit(solution)/shard_map/dot_general | solution.py:27
  58.4 0.0 copy-start.1
  58.4 0.0 copy-start.2
  58.4 0.0 copy-start.3
  58.4 0.0 reduce-scatter.2.cloned.1.call-update
  58.4 0.0 all-reduce.2.cloned.1.call-start
  58.5 90.7 %reduce-scatter.2.cloned.1.call-done = f32[896,128]{0,1:T(8,128)} async-done(((f32[14336,128]{0,1:T(8,128)}), f32[896,128]{0,1:T(8,128)}) %reduce-scatter.2.cloned.1.call-update) | async-done | bytes 458768 | tf_op jit(solution)/shard_map/reduce_scatter | solution.py:29
  149.2 0.0 all-reduce.2.cloned.1.call-update
  149.2 0.0 all-gather.5.cloned.1.call-start
  149.3 0.0 copy-done.1
  149.3 0.2 copy.8
  149.5 0.0 copy-done.2
  149.5 0.2 copy.9
  149.7 28.8 %all-reduce.2.cloned.1.call-done = f32[896,128]{0,1:T(8,128)} async-done(((f32[896,128]{0,1:T(8,128)}), f32[896,128]{0,1:T(8,128)}) %all-reduce.2.cloned.1.call-update) | async-done | bytes 458768 | tf_op jit(solution)/shard_map/psum | solution.py:28
  178.5 2.0 divide_convert_fusion
  180.5 0.0 all-gather.5.cloned.1.call-update
  180.5 1.0 copy.11
  181.5 1.0 copy.12
  182.4 46.4 %all-gather.5.cloned.1.call-done = bf16[14336,128]{0,1:T(8,128)(2,1)} async-done(((bf16[896,128]{0,1:T(8,128)(2,1)}), bf16[14336,128]{0,1:T(8,128)(2,1)}) %all-gather.5.cloned.1.call-update) | async-done | bytes 3670032 | tf_op jit(solution)/shard_map/all_gather | solution.py:34
  228.9 0.0 copy-done.3
  228.9 7.1 %fusion = bf16[256,14336]{0,1:T(8,128)(2,1)} fusion(bf16[14336,128]{0,1:T(8,128)(2,1)} %all-gather.5.cloned.1.call-done, bf16[256,128]{1,0:T(8,128)(2,1)S(1)} %copy-done.3), kind=kOutput, calls=%fused_computation.1 | convolution fusion | flops 943194112 | bytes 11075584 | tf_op jit(solution)/shard_map/dot_general | solution.py:32
  236.0 10.1 %copy.10 = bf16[256,14336]{1,0:T(8,128)(2,1)} copy(bf16[256,14336]{0,1:T(8,128)(2,1)} %fusion) | data formatting | bytes 14680064
Async XLA Ops:
  7.2 43.6 %copy-start = (bf16[192,4096]{1,0:T(8,128)(2,1)S(1)}, bf16[192,4096]{1,0:T(8,128)(2,1)}, u32[]{:S(2)}) copy-start(bf16[192,4096]{1,0:T(8,128)(2,1)} %param.5) | copy-start | bytes 4718596
  7.2 43.6 %all-gather.3.cloned.1.call-start = ((), (), s32[]{:S(2)}) async-start(), calls=%async_computation.1 | async-start | bytes 1114112 | tf_op jit(solution)/shard_map/all_gather | solution.py:23
  7.9 141.3 %reduce-scatter.2.cloned.1.call-start = ((), (), s32[]{:S(2)}) async-start(), calls=%async_computation.3 | async-start | bytes 7798784 | tf_op jit(solution)/shard_map/reduce_scatter | solution.py:29
  58.4 90.9 %copy-start.1 = (f32[896,128]{1,0:T(8,128)S(1)}, f32[896,128]{1,0:T(8,128)}, u32[]{:S(2)}) copy-start(f32[896,128]{1,0:T(8,128)} %param.8) | copy-start | bytes 1376260
  58.4 91.1 %copy-start.2 = (f32[896,128]{1,0:T(8,128)S(1)}, f32[896,128]{1,0:T(8,128)}, u32[]{:S(2)}) copy-start(f32[896,128]{1,0:T(8,128)} %param.9) | copy-start | bytes 1376260
  58.4 170.5 %copy-start.3 = (bf16[256,128]{1,0:T(8,128)(2,1)S(1)}, bf16[256,128]{1,0:T(8,128)(2,1)}, u32[]{:S(2)}) copy-start(bf16[256,128]{1,0:T(8,128)(2,1)} %param.7) | copy-start | bytes 196612
  58.4 120.1 %all-reduce.2.cloned.1.call-start = ((), (), s32[]{:S(2)}) async-start(), calls=%async_computation.4 | async-start | bytes 917504 | tf_op jit(solution)/shard_map/psum | solution.py:28
  149.2 79.6 %all-gather.5.cloned.1.call-start = ((), (), s32[]{:S(2)}) async-start(), calls=%async_computation.2 | async-start | bytes 3899392 | tf_op jit(solution)/shard_map/all_gather | solution.py:34
Sparse Core Ops, SparseCore 0:
  10.1 40.5 all-gather.2
  58.5 90.6 reduce-scatter.1
  151.5 26.9 all-reduce.1
  181.1 47.7 all-gather.4
where the time goes:
time: 253 us
  waiting for transfers between devices  209 us (83%)
  matrix products  14.7 us (6%)
  between operations  13.8 us (5%)
  local copies, waits for them, and re-layouts  12.5 us (5%)
    reduce_scatter x1, waiting for transfers between devices, local(): low_rank = lax.psum_scatter(whole, 'fsdp', scatter_dimension=0, tiled=True)  90.7 us
    all_gather x1, waiting for transfers between devices, local(): lax.all_gather(normalized, 'fsdp', axis=0, tiled=True)  46.4 us
    all_gather x1, waiting for transfers between devices, local(): lax.all_gather(projection, 'fsdp', axis=0, tiled=True)  42.8 us
    psum x1, waiting for transfers between devices, local(): whole = lax.psum(whole, 'dp')  28.8 us
    unnamed x13, local copies, waits for them, and re-layouts  12.5 us
    dot_general x1, matrix products, local(): lax.dot_general(grad_out, projected, contract, preferred_element_type=jnp...  7.64 us
    dot_general x1, matrix products, local(): lax.dot_general(projection, lax.all_gather(normalized, 'fsdp', axis=0, ti...  7.09 us
  transfers between devices with their start and end apart: 4, of which 4 were waited for; matrix products, arithmetic and copies ran while one was open for 1% of the time, Pallas kernels for 0%

commit v1 on v0

--- a/solution.py
+++ b/solution.py
@@ -25,7 +25,8 @@
     ).astype(jnp.bfloat16)
     contract = (((0,), (0,)), ((), ()))
     whole = lax.dot_general(grad_out, projected, contract, preferred_element_type=jnp.float32)
-    whole = lax.psum(whole, "dp")
+    later = lax.all_gather(whole, "dp")
+    whole = jnp.sum(later, axis=0)
     low_rank = lax.psum_scatter(whole, "fsdp", scatter_dimension=0, tiled=True)
     new_moment, new_second, normalized = adam_step(low_rank, moment, second)
     expand = (((1,), (1,)), ((), ()))

time: 253 us -> 439 us (1.74)
  waiting for transfers between devices: 209 us -> 355 us
  other arithmetic: 2.01 us -> 23.8 us
  local copies, waits for them, and re-layouts: 12.5 us -> 30.8 us
    all_gather x0 -> x1, waiting for transfers between devices: none -> 175 us  [local(): later = lax.all_gather(whole, 'dp')]
    psum x1 -> x0, waiting for transfers between devices: 28.8 us -> none  [local(): whole = lax.psum(whole, 'dp')]
    reduce_sum x0 -> x1, other arithmetic: none -> 21.8 us  [local(): whole = jnp.sum(later, axis=0)]
    all_gather x0 -> x1, local copies, waits for them, and re-layouts: none -> 17.4 us  [local(): later = lax.all_gather(whole, 'dp')]
    unnamed x13 -> x15, local copies, waits for them, and re-layouts: 12.5 us -> 13.4 us
where the time goes in v1:
time: 439 us; the launch traced here: 438 us
  waiting for transfers between devices  355 us (81%)
  local copies, waits for them, and re-layouts  30.8 us (7%)
  other arithmetic  23.8 us (5%)
  matrix products  14.8 us (3%)
  between operations  13.8 us (3%)
    all_gather x1, waiting for transfers between devices, local(): later = lax.all_gather(whole, 'dp')  175 us
    reduce_scatter x1, waiting for transfers between devices, local(): low_rank = lax.psum_scatter(whole, 'fsdp', scatter_dimension=0, tiled=True)  90.4 us
    all_gather x1, waiting for transfers between devices, local(): lax.all_gather(normalized, 'fsdp', axis=0, tiled=True)  46.1 us
    all_gather x1, waiting for transfers between devices, local(): lax.all_gather(projection, 'fsdp', axis=0, tiled=True)  42.8 us
    reduce_sum x1, other arithmetic, local(): whole = jnp.sum(later, axis=0)  21.8 us
    all_gather x1, local copies, waits for them, and re-layouts, local(): later = lax.all_gather(whole, 'dp')  17.4 us
    unnamed x15, local copies, waits for them, and re-layouts  13.4 us
  transfers between devices with their start and end apart: 4, of which 4 were waited for; matrix products, arithmetic and copies ran while one was open for 1% of the time, Pallas kernels for 0%

profile of v1, /device:TPU:0, one launch (start us, length us, event | category | flops | bytes accessed | tf_op | source)
XLA Modules:
  0.0 438.0 jit_solution(8605379560197742551)
XLA Ops:
  7.2 0.0 copy-start
  7.2 0.0 all-gather.5.cloned.1.call-start
  7.2 0.7 all-gather.5.cloned.1.call-update
  7.9 0.0 all-gather.9.cloned.1.call-start
  8.0 42.8 %all-gather.5.cloned.1.call-done = bf16[4096,128]{1,0:T(8,128)(2,1)} async-done(((bf16[256,128]{1,0:T(8,128)(2,1)}), bf16[4096,128]{1,0:T(8,128)(2,1)}) %all-gather.5.cloned.1.call-update) | async-done | bytes 1048592 | tf_op jit(solution)/shard_map/all_gather | solution.py:23
  50.7 0.0 copy-done
  50.7 7.6 %convolution_bitcast_fusion = f32[14336,128]{0,1:T(8,128)} fusion(bf16[192,14336]{1,0:T(8,128)(2,1)} %param.6, bf16[192,4096]{1,0:T(8,128)(2,1)S(1)} %copy-done, bf16[4096,128]{1,0:T(8,128)(2,1)} %all-gather.5.cloned.1.call-done), kind=kOutput, calls=%fused_computation.2 | convolution fusion | flops 905994240 | bytes 15466496 | tf_op jit(solution)/shard_map/dot_general | solution.py:27
  58.4 0.0 all-gather.9.cloned.1.call-update
  58.4 0.0 reduce-scatter.2.cloned.1.call-start
  58.5 174.5 %all-gather.9.cloned.1.call-done = f32[28672,128]{0,1:T(8,128)} async-done(((f32[14336,128]{0,1:T(8,128)}), f32[28672,128]{0,1:T(8,128)}) %all-gather.9.cloned.1.call-update) | async-done | bytes 14680080 | tf_op jit(solution)/shard_map/all_gather | solution.py:28
  233.0 17.4 %reshape.6 = f32[2,14336,128]{1,0,2:T(2,128)} reshape(f32[28672,128]{0,1:T(8,128)} %all-gather.9.cloned.1.call-done) | data formatting | bytes 29360128 | tf_op jit(solution)/shard_map/all_gather | solution.py:28
  250.4 21.8 %reduce_sum.9 = f32[14336,128]{0,1:T(8,128)} reduce(f32[2,14336,128]{1,0,2:T(2,128)} %reshape.6, f32[]{:T(128)} %constant.3.clone.1), dimensions={0}, to_apply=%region_0.0 | reduce | flops 1835008 | bytes 22020100 | tf_op jit(solution)/shard_map/reduce_sum | solution.py:29
  272.2 0.0 copy-start.2
  272.2 0.0 copy-start.3
  272.2 0.0 copy-start.4
  272.2 0.0 reduce-scatter.2.cloned.1.call-update
  272.2 0.0 all-gather.7.cloned.1.call-start
  272.3 0.9 copy-done.2
  273.2 0.2 copy.10
  273.4 0.0 copy-done.3
  273.4 0.2 copy.9
  273.6 90.4 %reduce-scatter.2.cloned.1.call-done = f32[896,128]{0,1:T(8,128)} async-done(((f32[14336,128]{0,1:T(8,128)}), f32[896,128]{0,1:T(8,128)}) %reduce-scatter.2.cloned.1.call-update) | async-done | bytes 458768 | tf_op jit(solution)/shard_map/reduce_scatter | solution.py:30
  364.0 2.0 divide_convert_fusion
  366.0 0.0 all-gather.7.cloned.1.call-update
  366.1 1.0 copy.12
  367.0 1.0 copy.13
  368.0 46.1 %all-gather.7.cloned.1.call-done = bf16[14336,128]{0,1:T(8,128)(2,1)} async-done(((bf16[896,128]{0,1:T(8,128)(2,1)}), bf16[14336,128]{0,1:T(8,128)(2,1)}) %all-gather.7.cloned.1.call-update) | async-done | bytes 3670032 | tf_op jit(solution)/shard_map/all_gather | solution.py:35
  414.1 0.0 copy-done.4
  414.1 0.0 copy-start.1
  414.2 7.2 %fusion = bf16[256,14336]{0,1:T(8,128)(2,1)} fusion(bf16[14336,128]{0,1:T(8,128)(2,1)} %all-gather.7.cloned.1.call-done, bf16[256,128]{1,0:T(8,128)(2,1)S(1)} %copy-done.4), kind=kOutput, calls=%fused_computation.1 | convolution fusion | flops 943194112 | bytes 11075584 | tf_op jit(solution)/shard_map/dot_general | solution.py:33
  421.4 10.1 %copy.11 = bf16[256,14336]{1,0:T(8,128)(2,1)} copy(bf16[256,14336]{0,1:T(8,128)(2,1)} %fusion) | data formatting | bytes 14680064
  431.5 0.0 copy-done.1
Async XLA Ops:
  7.2 43.6 %copy-start = (bf16[192,4096]{1,0:T(8,128)(2,1)S(1)}, bf16[192,4096]{1,0:T(8,128)(2,1)}, u32[]{:S(2)}) copy-start(bf16[192,4096]{1,0:T(8,128)(2,1)} %param.5) | copy-start | bytes 4718596
  7.2 43.6 %all-gather.5.cloned.1.call-start = ((), (), s32[]{:S(2)}) async-start(), calls=%async_computation.1 | async-start | bytes 1114112 | tf_op jit(solution)/shard_map/all_gather | solution.py:23
  7.9 225.1 %all-gather.9.cloned.1.call-start = ((), (), s32[]{:S(2)}) async-start(), calls=%async_computation.4 | async-start | bytes 22020096 | tf_op jit(solution)/shard_map/all_gather | solution.py:28
  58.4 305.6 %reduce-scatter.2.cloned.1.call-start = ((), (), s32[]{:S(2)}) async-start(), calls=%async_computation.2 | async-start | bytes 7798784 | tf_op jit(solution)/shard_map/reduce_scatter | solution.py:30
  272.2 1.0 copy-start.2
  272.2 1.2 copy-start.3
  272.2 141.9 %copy-start.4 = (bf16[256,128]{1,0:T(8,128)(2,1)S(1)}, bf16[256,128]{1,0:T(8,128)(2,1)}, u32[]{:S(2)}) copy-start(bf16[256,128]{1,0:T(8,128)(2,1)} %param.7) | copy-start | bytes 196612
  272.2 141.9 %all-gather.7.cloned.1.call-start = ((), (), s32[]{:S(2)}) async-start(), calls=%async_computation.3 | async-start | bytes 3899392 | tf_op jit(solution)/shard_map/all_gather | solution.py:35
  414.1 17.3 %copy-start.1 = (bf16[192,4096]{1,0:T(8,128)(2,1)S(1)}, bf16[192,4096]{1,0:T(8,128)(2,1)}, u32[]{:S(2)}) copy-start(bf16[192,4096]{1,0:T(8,128)(2,1)} %param.5) | copy-start | bytes 4718596
Sparse Core Ops, SparseCore 0:
  10.2 40.5 all-gather.4
  58.5 174.4 all-gather.8
  272.4 91.6 reduce-scatter.1
  366.6 47.4 all-gather.6
